TPU v7x, 32 devices: a whole 2x2x4 slice. The times are simulated.
32 devices in a mesh: seq: 8 (over y, x, core), head: 4 (over z).
Axes of the slice: x: 2, y: 2, z: 4, core: 2. Of those that a mesh axis runs over, the one named last changes fastest.
Arguments:
- hidden: bfloat16 [2, 4096, 1536], P(None, 'seq', 'head'), may hold values from -6 to 6
- norm_gain: float32 [1536], replicated, may hold values from 0.5 to 1.5
- gate_proj: bfloat16 [1536, 3072], P(None, 'head'), may hold values from -0.15625 to 0.15625
- value_proj: bfloat16 [1536, 3072], P(None, 'head'), may hold values from -0.15625 to 0.15625
- state_proj: bfloat16 [1536, 256], replicated, may hold values from -0.15625 to 0.15625
- step_proj: bfloat16 [1536, 48], P(None, 'head'), may hold values from -0.15625 to 0.15625
- conv_value: float32 [4, 3072], P(None, 'head'), may hold values from -3 to 3
- conv_value_bias: float32 [3072], P('head'), may hold values from -2 to 2
- conv_state: float32 [4, 256], replicated, may hold values from -3 to 3
- conv_state_bias: float32 [256], replicated, may hold values from -2 to 2
- step_bias: float32 [48], P('head'), may hold values from -4 to -1
- decay_log: float32 [48], P('head'), may hold values from -11 to 1
- skip_gain: float32 [48], P('head'), may hold values from 0.5 to 2
- gate_gain: float32 [3072], P('head'), may hold values from 0.5 to 1.5
- out_proj: bfloat16 [3072, 1536], P('head'), may hold values from -0.109375 to 0.109375
- cotangent: bfloat16 [2, 4096, 1536], P(None, 'seq', 'head'), may hold values from -6 to 6
Outputs:
- block_out: bfloat16 [2, 4096, 1536], P(None, 'seq', 'head')
- hidden_grad: bfloat16 [2, 4096, 1536], P(None, 'seq', 'head')
- norm_gain_grad: float32 [1536], P('head')
- gate_proj_grad: float32 [1536, 3072], P(None, 'head')
- value_proj_grad: float32 [1536, 3072], P(None, 'head')
- state_proj_grad: float32 [1536, 256], replicated
- step_proj_grad: float32 [1536, 48], P(None, 'head')
- conv_value_grad: float32 [4, 3072], P(None, 'head')
- conv_value_bias_grad: float32 [3072], P('head')
- conv_state_grad: float32 [4, 256], replicated
- conv_state_bias_grad: float32 [256], replicated
- step_bias_grad: float32 [48], P('head')
- decay_log_grad: float32 [48], P('head')
- skip_gain_grad: float32 [48], P('head')
- gate_gain_grad: float32 [3072], P('head')
- out_proj_grad: float32 [3072, 1536], P('head')
All inputs are finite; a program needn't handle non-finite values.
Results may differ from a plain program's by a relative error of at most 0.025.
The roundings to bfloat16 on the way count: a program that leaves them out, or rounds other values in their place, can miss the bound.
Values may be sent and summed in bfloat16 or wider, within the bound.
No kernel may reach another device: no remote copies, remote signals or barrier semaphores. Data moves between devices by JAX's collectives and lax.ppermute only.
A program may use at most 192 MiB of HBM per device.

v0:
```python
from functools import partial

import jax
import jax.numpy as jnp
from jax import lax
from jax.sharding import PartitionSpec as P

HEAD_DIM = 64
STATE = 128
CONV = 4
BLOCK = 256
INNER = 3072


EPS = 1e-05


def passed_along(block, axis, distance):
    devices = range(lax.axis_size(axis))
    route = [(i - distance, i) for i in devices if i - distance in devices]
    return lax.ppermute(block, axis, route)


def entering_2(shard, axis, combine, identity, reverse):
    size, index = (lax.axis_size(axis), lax.axis_index(axis))
    everything = jax.tree.map(lambda part: lax.all_gather(part, axis), shard)
    start = jax.tree.map(
        lambda part, zero: jnp.broadcast_to(jnp.asarray(zero, part.dtype), part.shape),
        shard,
        identity,
    )

    def turn(k, before):
        at = size - 1 - k if reverse else k
        reached = at > index if reverse else at < index
        new = combine(before, jax.tree.map(lambda part: part[at], everything))
        return jax.tree.map(lambda a, b: jnp.where(reached, a, b), new, before)

    return lax.fori_loop(0, size, turn, start)


def silu_grad(value):
    sigma = jax.nn.sigmoid(value)
    return sigma * (1.0 + value * (1.0 - sigma))


def decay_terms(step_raw, step_bias, decay_log):
    step_size = jax.nn.softplus(step_raw + step_bias)
    cumulative = jnp.cumsum(-jnp.exp(decay_log) * step_size, axis=1)
    return (jnp.swapaxes(cumulative, 1, 2), jnp.swapaxes(step_size, 1, 2))


def block_pieces(per_head, c_float, x_float, step_raw, step_bias, decay_log):
    cum_heads, step_heads = decay_terms(step_raw, step_bias, decay_log)
    span = cum_heads.shape[-1]
    causal_mask = jnp.tril(jnp.ones((span, span), dtype=bool))
    spread = cum_heads[..., :, None] - cum_heads[..., None, :]
    damping = jnp.where(causal_mask, jnp.exp(jnp.where(causal_mask, spread, 0.0)), 0.0)
    mixing = per_head * damping * step_heads[..., None, :]
    c_scaled = jnp.exp(cum_heads)[..., None] * c_float[:, None]
    block_total = cum_heads[..., -1]
    weights = jnp.exp(block_total[..., None] - cum_heads) * step_heads
    x_weighted = x_float * jnp.swapaxes(weights, 1, 2)[..., None]
    return (mixing, c_scaled, x_weighted, block_total)


def per_head_scores(c_blocks, b_blocks, head_count):
    scores = jnp.einsum("cqn,csn->cqs", c_blocks, b_blocks, preferred_element_type=jnp.float32)
    return jnp.broadcast_to(scores[:, None], (scores.shape[0], head_count) + scores.shape[1:])


def device_state(inputs, step_bias, decay_log):
    x_blocks, b_blocks, raw_blocks = inputs
    cum_heads, step_heads = decay_terms(raw_blocks, step_bias, decay_log)
    block_total = cum_heads[..., -1]
    weights = jnp.exp(block_total[..., None] - cum_heads) * step_heads
    x_weighted = (x_blocks.astype(jnp.float32) * jnp.swapaxes(weights, 1, 2)[..., None]).astype(
        jnp.bfloat16
    )
    local_states = jnp.einsum(
        "cqhp,cqn->chpn", x_weighted, b_blocks, preferred_element_type=jnp.float32
    )

    def advance(carry_state, pair):
        factor, term = pair
        return (jnp.exp(factor)[:, None, None] * carry_state + term, None)

    final_state, _ = lax.scan(
        advance, jnp.zeros(local_states.shape[1:], jnp.float32), (block_total, local_states)
    )
    return (jnp.exp(jnp.sum(block_total, 0)), final_state, local_states)


def device_output(inputs, step_bias, decay_log, skip_gain):
    x_blocks, b_blocks, c_blocks, raw_blocks, local_states, entering = inputs
    per_head = per_head_scores(c_blocks, b_blocks, x_blocks.shape[2])
    x_float = x_blocks.astype(jnp.float32)
    mixing, c_scaled, _, block_total = block_pieces(
        per_head, c_blocks.astype(jnp.float32), x_float, raw_blocks, step_bias, decay_log
    )

    def advance(carry_state, pair):
        factor, term = pair
        return (jnp.exp(factor)[:, None, None] * carry_state + term, carry_state)

    _, starts = lax.scan(advance, entering, (block_total, local_states))
    inside = jnp.einsum(
        "chts,cshp->cthp", mixing.astype(jnp.bfloat16), x_blocks, preferred_element_type=jnp.float32
    )
    carried = jnp.einsum(
        "chtn,chpn->cthp",
        c_scaled.astype(jnp.bfloat16),
        starts.astype(jnp.bfloat16),
        preferred_element_type=jnp.float32,
    )
    return (inside + carried + skip_gain[:, None] * x_float, starts)


def device_sensitivity(inputs, step_bias, decay_log):
    c_blocks, raw_blocks, grad_blocks = inputs
    cum_heads, _ = decay_terms(raw_blocks, step_bias, decay_log)
    c_scaled = (jnp.exp(cum_heads)[..., None] * c_blocks.astype(jnp.float32)[:, None]).astype(
        jnp.bfloat16
    )
    state_grads = jnp.einsum(
        "cthp,chtn->chpn", grad_blocks, c_scaled, preferred_element_type=jnp.float32
    )

    def retreat(carry_grad, pair):
        factor, term = pair
        return (jnp.exp(factor)[:, None, None] * carry_grad + term, None)

    sensitivity, _ = lax.scan(
        retreat,
        jnp.zeros(state_grads.shape[1:], jnp.float32),
        (cum_heads[..., -1], state_grads),
        reverse=True,
    )
    return (sensitivity, state_grads)


def device_backward(inputs, step_bias, decay_log, skip_gain):
    x_blocks, b_blocks, c_blocks, raw_blocks, grad_blocks, starts, state_grads, leaving = inputs
    per_head = per_head_scores(c_blocks, b_blocks, x_blocks.shape[2])
    x_float = x_blocks.astype(jnp.float32)
    pieces, pullback = jax.vjp(
        block_pieces,
        per_head,
        c_blocks.astype(jnp.float32),
        x_float,
        raw_blocks,
        step_bias,
        decay_log,
    )
    mixing, c_scaled, x_weighted, block_total = pieces

    def retreat(carry_grad, triple):
        factor, term, start_state = triple
        return (
            jnp.exp(factor)[:, None, None] * carry_grad + term,
            (carry_grad, jnp.sum(carry_grad * start_state, (1, 2))),
        )

    _, (end_grads, factor_grads) = lax.scan(
        retreat, leaving, (block_total, state_grads, starts), reverse=True
    )
    end_low = end_grads.astype(jnp.bfloat16)
    grad_mixing = jnp.einsum(
        "cthp,cshp->chts", grad_blocks, x_blocks, preferred_element_type=jnp.float32
    )
    grad_x = jnp.einsum(
        "chts,cthp->cshp",
        mixing.astype(jnp.bfloat16),
        grad_blocks,
        preferred_element_type=jnp.float32,
    )
    grad_scaled = jnp.einsum(
        "cthp,chpn->chtn",
        grad_blocks,
        starts.astype(jnp.bfloat16),
        preferred_element_type=jnp.float32,
    )
    grad_weighted = jnp.einsum(
        "csn,chpn->cshp", b_blocks, end_low, preferred_element_type=jnp.float32
    )
    grad_b = jnp.einsum(
        "cshp,chpn->csn",
        x_weighted.astype(jnp.bfloat16),
        end_low,
        preferred_element_type=jnp.float32,
    )
    grad_head, grad_c, grad_piece_x, grad_raw, grad_bias, grad_decay = pullback(
        (grad_mixing, grad_scaled, grad_weighted, factor_grads * jnp.exp(block_total))
    )
    score_low = grad_head.astype(jnp.bfloat16)
    grad_c = grad_c + jnp.einsum(
        "chts,csn->ctn", score_low, b_blocks, preferred_element_type=jnp.float32
    )
    grad_b = grad_b + jnp.einsum(
        "chts,ctn->csn", score_low, c_blocks, preferred_element_type=jnp.float32
    )
    grad_float = grad_blocks.astype(jnp.float32)
    grad_x = grad_x + grad_piece_x + skip_gain[:, None] * grad_float
    grad_skip = jnp.sum(grad_float * x_float, (0, 1, 3))
    return (grad_x, grad_b, grad_c, grad_raw, grad_bias, grad_decay, grad_skip)


def combine_states(earlier, later):
    return (earlier[0] * later[0], later[0][..., None, None] * earlier[1] + later[1])


def body(
    hidden,
    norm_gain,
    gate_proj,
    value_proj,
    state_proj,
    step_proj,
    conv_value,
    conv_value_bias,
    conv_state,
    conv_state_bias,
    step_bias,
    decay_log,
    skip_gain,
    gate_gain,
    out_proj,
    cotangent,
):
    batch, tokens, part_width = hidden.shape
    head_index = lax.axis_index("head")
    inner_local = value_proj.shape[1]
    head_local = step_proj.shape[1]
    blocks = tokens // BLOCK
    full_rows = lax.all_gather(hidden, "head", axis=2, tiled=True)
    rows_float = full_rows.astype(jnp.float32)
    inv_rms = lax.rsqrt(jnp.mean(rows_float * rows_float, -1, keepdims=True) + EPS)
    unit_rows = rows_float * inv_rms
    normed = (unit_rows * norm_gain).astype(jnp.bfloat16)
    in_weights = jnp.concatenate([value_proj, state_proj], 1)
    gate_in = jnp.einsum("btd,de->bte", normed, gate_proj, preferred_element_type=jnp.float32)
    conv_in = jnp.einsum("btd,de->bte", normed, in_weights, preferred_element_type=jnp.float32)
    step_raw = jnp.einsum("btd,de->bte", normed, step_proj, preferred_element_type=jnp.float32)
    edge = passed_along(conv_in[:, tokens - (CONV - 1) :], "seq", 1)
    extended = jnp.concatenate([edge, conv_in], 1)
    kernel = jnp.concatenate([conv_value, conv_state], 1)
    kernel_bias = jnp.concatenate([conv_value_bias, conv_state_bias])

    def convolve(source, taps, offsets):
        return jax.nn.silu(
            offsets
            + sum(
                (
                    taps[position] * source[:, position : position + tokens]
                    for position in range(CONV)
                )
            )
        )

    activated, conv_pull = jax.vjp(convolve, extended, kernel, kernel_bias)
    x_blocks = (
        activated[..., :inner_local]
        .astype(jnp.bfloat16)
        .reshape(batch, blocks, BLOCK, head_local, HEAD_DIM)
    )
    b_blocks = (
        activated[..., inner_local : inner_local + STATE]
        .astype(jnp.bfloat16)
        .reshape(batch, blocks, BLOCK, STATE)
    )
    c_blocks = (
        activated[..., inner_local + STATE :]
        .astype(jnp.bfloat16)
        .reshape(batch, blocks, BLOCK, STATE)
    )
    raw_blocks = step_raw.reshape(batch, blocks, BLOCK, head_local)
    decay_device, state_device, local_states = lax.map(
        partial(device_state, step_bias=step_bias, decay_log=decay_log),
        (x_blocks, b_blocks, raw_blocks),
    )
    identity = (jnp.ones_like(decay_device), jnp.zeros_like(state_device))
    entering = entering_2((decay_device, state_device), "seq", combine_states, identity, False)
    outputs, starts = lax.map(
        partial(device_output, step_bias=step_bias, decay_log=decay_log, skip_gain=skip_gain),
        (x_blocks, b_blocks, c_blocks, raw_blocks, local_states, entering[1]),
    )
    ssd_out = outputs.reshape(batch, tokens, inner_local)
    gate_act = jax.nn.silu(gate_in)
    gated = ssd_out * gate_act
    square_sum = lax.psum(jnp.sum(gated * gated, -1), "head")
    inv_gate = lax.rsqrt(square_sum[..., None] / INNER + EPS)
    unit_gated = gated * inv_gate
    normal_gated = (unit_gated * gate_gain).astype(jnp.bfloat16)
    partial_out = jnp.einsum(
        "btk,kd->btd", normal_gated, out_proj, preferred_element_type=jnp.float32
    )
    out_part = lax.psum_scatter(
        partial_out.astype(jnp.bfloat16), "head", scatter_dimension=2, tiled=True
    ).astype(jnp.float32)
    block_out = (hidden.astype(jnp.float32) + out_part).astype(jnp.bfloat16)
    grad_out_rows = lax.all_gather(cotangent, "head", axis=2, tiled=True)
    out_proj_grad = jnp.einsum(
        "btk,btd->kd", normal_gated, grad_out_rows, preferred_element_type=jnp.float32
    )
    grad_normal = jnp.einsum(
        "btd,kd->btk", grad_out_rows, out_proj, preferred_element_type=jnp.float32
    )
    gate_gain_grad = jnp.sum(grad_normal * unit_gated, (0, 1))
    grad_unit = grad_normal * gate_gain
    unit_dot = lax.psum(jnp.sum(grad_unit * unit_gated, -1), "head")
    grad_gated = inv_gate * (grad_unit - unit_gated * unit_dot[..., None] / INNER)
    grad_ssd = (grad_gated * gate_act).astype(jnp.bfloat16)
    grad_gate_in = (grad_gated * ssd_out * silu_grad(gate_in)).astype(jnp.bfloat16)
    grad_blocks = grad_ssd.reshape(batch, blocks, BLOCK, head_local, HEAD_DIM)
    sensitivity, state_grads = lax.map(
        partial(device_sensitivity, step_bias=step_bias, decay_log=decay_log),
        (c_blocks, raw_blocks, grad_blocks),
    )
    leaving = entering_2((decay_device, sensitivity), "seq", combine_states, identity, True)
    grad_x, grad_b, grad_c, grad_raw, grad_bias_each, grad_decay_each, grad_skip_each = lax.map(
        partial(device_backward, step_bias=step_bias, decay_log=decay_log, skip_gain=skip_gain),
        (x_blocks, b_blocks, c_blocks, raw_blocks, grad_blocks, starts, state_grads, leaving[1]),
    )
    shared = lax.psum(
        jnp.concatenate(
            [grad_b.reshape(batch, tokens, STATE), grad_c.reshape(batch, tokens, STATE)], -1
        ).astype(jnp.bfloat16),
        "head",
    ).astype(jnp.float32)
    grad_activated = jnp.concatenate([grad_x.reshape(batch, tokens, inner_local), shared], -1)
    grad_extended, kernel_grad, kernel_bias_grad = conv_pull(grad_activated)
    returned = passed_along(grad_extended[:, : CONV - 1], "seq", -1)
    grad_conv_in = grad_extended[:, CONV - 1 :].at[:, tokens - (CONV - 1) :].add(returned)
    grad_conv_low = grad_conv_in.astype(jnp.bfloat16)
    grad_raw_low = grad_raw.reshape(batch, tokens, head_local).astype(jnp.bfloat16)
    gate_proj_grad = jnp.einsum(
        "btd,bte->de", normed, grad_gate_in, preferred_element_type=jnp.float32
    )
    in_grad = jnp.einsum("btd,bte->de", normed, grad_conv_low, preferred_element_type=jnp.float32)
    step_proj_grad = jnp.einsum(
        "btd,bte->de", normed, grad_raw_low, preferred_element_type=jnp.float32
    )
    owner = (head_index == 0).astype(jnp.bfloat16)
    back_weights = jnp.concatenate([value_proj, state_proj * owner], 1)
    grad_normed = jnp.einsum(
        "bte,de->btd", grad_gate_in, gate_proj, preferred_element_type=jnp.float32
    )
    grad_normed = grad_normed + jnp.einsum(
        "bte,de->btd", grad_conv_low, back_weights, preferred_element_type=jnp.float32
    )
    grad_normed = grad_normed + jnp.einsum(
        "bte,de->btd", grad_raw_low, step_proj, preferred_element_type=jnp.float32
    )
    grad_full = lax.psum(grad_normed.astype(jnp.bfloat16), "head").astype(jnp.float32)
    gain_full = jnp.sum(grad_full * unit_rows, (0, 1))
    norm_gain_grad = lax.dynamic_slice_in_dim(gain_full, head_index * part_width, part_width)
    grad_unit_rows = grad_full * norm_gain
    inner_dot = jnp.mean(grad_unit_rows * unit_rows, -1, keepdims=True)
    grad_rows_full = inv_rms * (grad_unit_rows - unit_rows * inner_dot)
    grad_input = lax.dynamic_slice_in_dim(grad_rows_full, head_index * part_width, part_width, 2)
    hidden_grad = (cotangent.astype(jnp.float32) + grad_input).astype(jnp.bfloat16)
    totals = lax.psum(
        (
            norm_gain_grad,
            gate_proj_grad,
            in_grad,
            step_proj_grad,
            kernel_grad,
            kernel_bias_grad,
            jnp.sum(grad_bias_each, 0),
            jnp.sum(grad_decay_each, 0),
            jnp.sum(grad_skip_each, 0),
            gate_gain_grad,
            out_proj_grad,
        ),
        "seq",
    )
    return (
        block_out,
        hidden_grad,
        totals[0],
        totals[1],
        totals[2][:, :inner_local],
        totals[2][:, inner_local:],
        totals[3],
        totals[4][:, :inner_local],
        totals[5][:inner_local],
        totals[4][:, inner_local:],
        totals[5][inner_local:],
        totals[6],
        totals[7],
        totals[8],
        totals[9],
        totals[10],
    )


def solution(mesh):
    placed = (
        P(None, "seq", "head"),
        P(),
        P(None, "head"),
        P(None, "head"),
        P(),
        P(None, "head"),
        P(None, "head"),
        P("head"),
        P(),
        P(),
        P("head"),
        P("head"),
        P("head"),
        P("head"),
        P("head", None),
        P(None, "seq", "head"),
    )
    return jax.shard_map(
        body,
        mesh=mesh,
        in_specs=placed,
        out_specs=(
            P(None, "seq", "head"),
            P(None, "seq", "head"),
            P("head"),
            P(None, "head"),
            P(None, "head"),
            P(),
            P(None, "head"),
            P(None, "head"),
            P("head"),
            P(),
            P(),
            P("head"),
            P("head"),
            P("head"),
            P("head"),
            P("head", None),
        ),
        check_vma=False,
    )
```

profile of v0, /device:TPU:0, one launch (start us, length us, event | category | flops | bytes accessed | tf_op | source)
XLA Modules:
  0.0 948.8 jit_solution(6586396444774847396)
XLA Ops:
  11.4 64.2 %all-gather.9.cloned.1.call-done = bf16[2,512,1536]{2,1,0:T(8,128)(2,1)} async-done(((bf16[2,512,384]{2,1,0:T(8,128)(2,1)}), bf16[2,512,1536]{2,1,0:T(8,128)(2,1)}) %all-gather.9.cloned.1.call-update) | async-done | bytes 3145744 | tf_op jit(solution)/shard_map/all_gather | solution.py:235
  88.9 9.2 multiply_convert_fusion.14
  112.1 17.8 %while.202 = (s32[]{:T(128)}, f32[2,12]{1,0:T(2,128)}, f32[2,12,64,128]{3,2,1,0:T(8,128)}, f32[2,2,12,64,128]{4,3,2,1,0:T(8,128)}, f32[1,1,12]{2,1,0:T(1,128)S(1...) while((s32[]{:T(128)}, f32[2,12]{1,0:T(2,128)}, ...), condition=%wide.region_7.8_spmd, body=%wide.region_1.7_spmd.sunk | while | flops 102985816 | bytes 4977476 | solution.py:277
  130.8 11.9 %all-gather.3 = f32[8,2,12]{2,1,0:T(2,128)S(1)} all-gather(f32[1,2,12]{2,1,0:T(2,128)} %bitcast.594), channel_id=2, replica_groups=mesh['seq'=8,'head'=4] {'seq'}, dimensions={0}, use_global_device_ids=true | all-gather | bytes 864 | tf_op jit(solution)/shard_map/all_gather | solution.py:26
  142.7 33.4 %all-gather.13.cloned.1.call-done = f32[16,12,64,128]{3,2,1,0:T(8,128)} async-done(((f32[2,12,64,128]{3,2,1,0:T(8,128)}), f32[16,12,64,128]{3,2,1,0:T(8,128)}) %all-gather.13.cloned.1.call-update) | async-done | bytes 6291472 | tf_op jit(solution)/shard_map/all_gather | solution.py:26
  176.0 10.8 %while.209 = (s32[]{:T(128)}, f32[2,12,64,128]{3,2,1,0:T(8,128)S(1)}, s32[]{:T(128)}, f32[8,2,12]{2,1,0:T(2,128)S(1)}, f32[8,2,12,64,128]{4,3,2,1,0:T(8,128)}, /*index=5*/s32[]{:T(128)}, s32[]{:T(128)}) while((s32[]{:T(128)}, f32[2,12,64,128]{3,2,1,0:T(8,128)S(1)}, s32[]{:T(128)}, f32[8,2,12]{2,1,0:T(2,128)S(1)}, ...), condition=%wide.region_9.10_spmd.clone, body=%wide.region_8.9_spmd.clone.sunk | while | flops 786436 | bytes 2359689 | solution.py:39
  191.3 43.0 %while.204 = (s32[]{:T(128)}, f32[2,2,256,12,64]{2,1,4,3,0:T(2,128)}, f32[2,2,12,64,128]{4,3,2,1,0:T(8,128)}, bf16[2,2,256,12,64]{2,4,3,1,0:T(8,128)(2,1)}, bf16...) while((s32[]{:T(128)}, ...), condition=%wide.region_15.16_spmd, body=%wide.region_10.15_spmd.sunk | while | flops 349487168 | bytes 53613600 | solution.py:283
  243.4 8.4 multiply_reduce_fusion.10
  251.8 11.7 %psum.105 = f32[2,512]{1,0:T(2,128)S(1)} all-reduce(f32[2,512]{1,0:T(2,128)S(1)} %get-tuple-element.1882), channel_id=1, replica_groups=mesh['seq'=8,'head'=4] {'head'}, use_global_device_ids=true, to_apply=%region_17.18 | all-reduce | flops 1024 | bytes 8192 | tf_op jit(solution)/shard_map/psum | solution.py:290
  263.6 8.7 multiply_reduce_fusion.8
  272.2 8.3 psum.106
  298.6 15.6 %while.206 = (s32[]{:T(128)}, f32[2,12,64,128]{3,2,1,0:T(8,128)}, f32[2,2,12,64,128]{4,3,2,1,0:T(8,128)}, f32[1,1,12]{2,1,0:T(1,128)S(1)}, f32[2,2,256,12]{2,1,3...) while((s32[]{:T(128)}, f32[2,12,64,128]{3,2,1,0:T(8,128)}, ...), condition=%wide.region_26.27_spmd, body=%wide.region_21.26_spmd.sunk | while | flops 103432272 | bytes 5451576 | solution.py:315
  314.3 44.1 %all-gather.15.cloned.1.call-done = f32[16,12,64,128]{3,2,1,0:T(8,128)} async-done(((f32[2,12,64,128]{3,2,1,0:T(8,128)}), f32[16,12,64,128]{3,2,1,0:T(8,128)}) %all-gather.15.cloned.1.call-update) | async-done | bytes 6291472 | tf_op jit(solution)/shard_map/all_gather | solution.py:26
  358.5 16.0 %while.210 = (s32[]{:T(128)}, f32[2,12,64,128]{3,2,1,0:T(8,128)S(1)}, s32[]{:T(128)}, f32[8,2,12]{2,1,0:T(2,128)}, f32[8,2,12,64,128]{4,3,2,1,0:T(8,128)}, /*index=5*/s32[]{:T(128)}, s32[]{:T(128)}, s32[]{:T(128)}, s32[]{:T(128)}) while((s32[]{:T(128)}, f32[2,12,64,128]{3,2,1,0:T(8,128)S(1)}, s32[]{:T(128)}, ...), condition=%wide.region_28.29_spmd.clone, body=%wide.region_27.28_spmd.clone.sunk | while | flops 786440 | bytes 2359751 | solution.py:39
  379.3 109.3 %while.208 = (s32[]{:T(128)}, f32[2,2,256,12,64]{2,1,4,3,0:T(2,128)}, bf16[2,2,256,128]{3,2,1,0:T(8,128)(2,1)}, bf16[2,2,256,128]{3,2,1,0:T(8,128)(2,1)}, bf16[2...) while((s32[]{:T(128)}, ...), condition=%wide.region_48.49_spmd, body=%wide.region_29.48_spmd.sunk | while | flops 852496512 | bytes 79454616 | solution.py:320
  497.7 8.7 copy.301
  532.8 12.3 %multiply_reduce_fusion.6 = (f32[1024]{0:T(1024)S(1)}, f32[1024]{0:T(1024)S(1)}, f32[1024]{0:T(1024)S(1)}, f32[1024]{0:T(1024)S(1)}, f32[1024]{0:T(1024)S(1)}, /*index=5*/f32[2,512,1024]{2,1,0:T(8,128)}) fusion(f32[2,512,1024]{2,1,0:T(8,128)} %copy-done.10, f32[2,3,1024]{2,1,0:T(4,128)S(1)} %copy-done.45, f32[2,512,1024]{2,1,0:T(8,128)} %get-tuple-element.1885, ...), kind=kLoop, calls=%fused_computation.234 | loop fusion | flops 23063552 | bytes 16822272 | tf_op jit(solution)/shard_map/transpose(jvp())/reduce_sum | solution.py:254
  545.2 7.8 broadcast_multiply_fusion
  566.1 11.1 %add_convert_fusion = bf16[2,512,1536]{2,1,0:T(8,128)(2,1)} fusion(f32[2,512,1536]{2,1,0:T(8,128)} %fusion.148, f32[2,512,1536]{2,1,0:T(8,128)} %fusion.138, bf16[1536,768]{1,0:T(8,128)(2,1)} %param.41, bf16[1536,256]{1,0:T(8,128)(2,1)S(1)} %copy-done.38, bf16[2,512,1024]{2,1,0:T(8,128)(2,1)} %scatter-add.4), kind=kOutput, calls=%fused_computation.219 | convolution fusion | flops 3232235520 | bytes 20971520 | tf_op jit(solution)/shard_map/bte,de->btd/dot_general | solution.py:348
  577.9 7.6 convolution_bitcast_fusion.3
  604.3 111.4 %all-reduce.17.cloned.1.call-done = bf16[2,512,1536]{2,1,0:T(8,128)(2,1)} async-done(((bf16[2,512,1536]{2,1,0:T(8,128)(2,1)}), bf16[2,512,1536]{2,1,0:T(8,128)(2,1)}) %all-reduce.17.cloned.1.call-update) | async-done | bytes 3145744 | tf_op jit(solution)/shard_map/psum | solution.py:354
  715.7 7.6 fusion.122
  723.4 26.2 %all-reduce.9 = (f32[384]{0:T(512)}, f32[4,1024]{1,0:T(4,128)S(1)}, f32[1024]{0:T(1024)S(1)}, f32[12]{0:T(128)}, f32[12]{0:T(128)}, /*index=5*/f32[12]{0:T(128)}, f32[768]{0:T(1024)}) all-reduce(f32[384]{0:T(512)S(1)} %dynamic_slice.243, f32[4,1024]{1,0:T(4,128)S(1)} %pad_add_fusion.2, ...), channel_id=1, replica_groups=mesh['seq'=8,'head'=4] {'seq'}, use_global_device_ids=true, to_apply=%region_53.54 | all-reduce | flops 6308 | bytes 50464 | tf_op jit(solution)/shard_map/psum | solution.py:362
  754.6 173.2 %all-reduce.19.cloned.1.call-done = (f32[1536,768]{1,0:T(8,128)}, f32[1536,1024]{1,0:T(8,128)}, f32[1536,12]{0,1:T(8,128)}, f32[768,1536]{1,0:T(8,128)}) async-done(((f32[1536,768]{1,0:T(8,128)}, f32[1536,1024]{1,0:T(8,128)}, f32[1536,12]{0,1:T(8,128)}, f32[768,1536]{1,0:T(8,128)}), (f32[1536,768]{1,0:T(8,128)}, f32[1536,1024]{1,0:T(8,128)}, f32[1536,12]{0,1:T(8,128)}, ...) | async-done | bytes 15802384 | tf_op jit(solution)/shard_map/psum | solution.py:362
  (629 shorter events, 382.9 us)
Async XLA Ops:
  7.2 236.2 %copy-start = (bf16[1536,768]{1,0:T(8,128)(2,1)S(1)}, bf16[1536,768]{1,0:T(8,128)(2,1)}, u32[]{:S(2)}) copy-start(bf16[1536,768]{1,0:T(8,128)(2,1)} %param.40) | copy-start | bytes 7077892
  7.2 71.1 %copy-start.64 = (f32[1536]{0:T(1024)S(1)}, f32[1536]{0:T(1024)}, u32[]{:S(2)}) copy-start(f32[1536]{0:T(1024)} %param.39) | copy-start | bytes 18436
  7.2 71.1 %copy-start.36 = (bf16[1536,256]{1,0:T(8,128)(2,1)S(1)}, bf16[1536,256]{1,0:T(8,128)(2,1)}, u32[]{:S(2)}) copy-start(bf16[1536,256]{1,0:T(8,128)(2,1)} %param.42) | copy-start | bytes 2359300
  7.2 68.4 %all-gather.9.cloned.1.call-start = ((), (), s32[]{:S(2)}) async-start(), calls=%async_computation.1 | async-start | bytes 3932160 | tf_op jit(solution)/shard_map/all_gather | solution.py:235
  8.0 168.1 %all-gather.13.cloned.1.call-start = ((), (), s32[]{:S(2)}) async-start(), calls=%async_computation.5 | async-start | bytes 7077888 | tf_op jit(solution)/shard_map/all_gather | solution.py:26
  11.4 77.5 %copy-start.54 = (f32[1,1024]{1,0:T(1,128)}, f32[1,1024]{1,0:T(1,128)S(1)}, u32[]{:S(2)}) copy-start(f32[1,1024]{1,0:T(1,128)S(1)} %get-tuple-element.1915) | copy-start | bytes 12292
  11.4 77.5 %copy-start.56 = (f32[1,1024]{1,0:T(1,128)}, f32[1,1024]{1,0:T(1,128)S(1)}, u32[]{:S(2)}) copy-start(f32[1,1024]{1,0:T(1,128)S(1)} %get-tuple-element.1916) | copy-start | bytes 12292
  11.4 77.5 %copy-start.58 = (f32[1,1024]{1,0:T(1,128)}, f32[1,1024]{1,0:T(1,128)S(1)}, u32[]{:S(2)}) copy-start(f32[1,1024]{1,0:T(1,128)S(1)} %get-tuple-element.1917) | copy-start | bytes 12292
  11.4 77.5 %copy-start.60 = (f32[1,1024]{1,0:T(1,128)}, f32[1,1024]{1,0:T(1,128)S(1)}, u32[]{:S(2)}) copy-start(f32[1,1024]{1,0:T(1,128)S(1)} %get-tuple-element.1918) | copy-start | bytes 12292
  85.6 3.3 collective-permute-start
  130.0 133.6 %all-gather.11.cloned.1.call-start = ((), (), s32[]{:S(2)}) async-start(), calls=%async_computation.2 | async-start | bytes 3932160 | tf_op jit(solution)/shard_map/all_gather | solution.py:301
  130.7 227.8 %all-gather.15.cloned.1.call-start = ((), (), s32[]{:S(2)}) async-start(), calls=%async_computation.6 | async-start | bytes 7077888 | tf_op jit(solution)/shard_map/all_gather | solution.py:26
  243.4 20.2 %copy-start.42 = (f32[768]{0:T(1024)S(1)}, f32[768]{0:T(1024)}, u32[]{:S(2)}) copy-start(f32[768]{0:T(1024)} %param.51) | copy-start | bytes 9220
  263.5 17.0 %copy-start.40 = (f32[2,512]{1,0:T(2,128)}, f32[2,512]{1,0:T(2,128)S(1)}, u32[]{:S(2)}) copy-start(f32[2,512]{1,0:T(2,128)S(1)} %add_rsqrt_fusion) | copy-start | bytes 12292
  314.2 217.4 %all-reduce.15.cloned.1.call-start = ((), (), s32[]{:S(2)}) async-start(), calls=%async_computation.3 | async-start | bytes 1048576 | tf_op jit(solution)/shard_map/psum | solution.py:324
  409.1 14.4 %copy-start.8 = (bf16[2,12,64,128]{3,2,1,0:T(8,128)(2,1)S(1)}, bf16[2,12,64,128]{3,2,1,0:T(8,128)(2,1)}, u32[]{:S(2)}) copy-start(bf16[2,12,64,128]{3,2,1,0:T(8,128)(2,1)} %get-tuple-element.2477) | copy-start | bytes 1179652 | tf_op jit(solution)/shard_map/while
  463.5 14.4 %copy-start.8 = (bf16[2,12,64,128]{3,2,1,0:T(8,128)(2,1)S(1)}, bf16[2,12,64,128]{3,2,1,0:T(8,128)(2,1)}, u32[]{:S(2)}) copy-start(bf16[2,12,64,128]{3,2,1,0:T(8,128)(2,1)} %get-tuple-element.2477) | copy-start | bytes 1179652 | tf_op jit(solution)/shard_map/while
  490.5 106.8 %reduce-scatter.4.cloned.1.call-start = ((), (), s32[]{:S(2)}) async-start(), calls=%async_computation.7 | async-start | bytes 3932160
  510.8 204.9 %all-reduce.17.cloned.1.call-start = ((), (), s32[]{:S(2)}) async-start(), calls=%async_computation.4 | async-start | bytes 6291456 | tf_op jit(solution)/shard_map/psum | solution.py:354
  553.9 8.9 collective-permute-start.1
  577.3 350.5 %all-reduce.19.cloned.1.call-start = ((), (), s32[]{:S(2)}) async-start(), calls=%async_computation.8 | async-start | bytes 31653888 | tf_op jit(solution)/shard_map/psum | solution.py:362
  604.2 119.1 %copy-start.67 = (f32[768]{0:T(1024)S(1)}, f32[768]{0:T(1024)}, u32[]{:S(2)}) copy-start(f32[768]{0:T(1024)} %get-tuple-element.1701) | copy-start | bytes 9220
  604.3 147.1 %copy-start.24 = (bf16[2,512,384]{2,1,0:T(8,128)(2,1)S(1)}, bf16[2,512,384]{2,1,0:T(8,128)(2,1)}, u32[]{:S(2)}) copy-start(bf16[2,512,384]{2,1,0:T(8,128)(2,1)} %param.53) | copy-start | bytes 2359300
  749.6 183.2 %copy-start.73 = (f32[1024]{0:T(1024)}, f32[1024]{0:T(1024)S(1)}, u32[]{:S(2)}) copy-start(f32[1024]{0:T(1024)S(1)} %get-tuple-element.1866) | copy-start | bytes 12292
  (95 other events, 471.2 us)
Sparse Core Ops, SparseCore 0:
  9.6 65.9 all-gather.8
  130.1 45.9 all-gather.12
  177.6 63.2 all-gather.10
  314.4 44.0 all-gather.14
  490.6 38.6 all-reduce.14
  532.1 60.2 reduce-scatter.3
  594.7 120.9 all-reduce.16
  721.2 206.5 all-reduce.18
where the time goes:
time: 959 us; the launch traced here: 949 us
  waiting for transfers between devices  428 us (45%)
  local copies, waits for them, and re-layouts  165 us (17%)
  matrix products  145 us (15%)
  other arithmetic  132 us (14%)
  blocking collectives  58.2 us (6%)
  between operations  14.9 us (2%)
    psum x1, waiting for transfers between devices, body(): lax.psum((norm_gain_grad, gate_proj_grad, in_grad, step_proj_grad, kernel...  173 us
    psum x1, waiting for transfers between devices, body(): lax.psum(grad_normed.astype(jnp.bfloat16), 'head').astype(jnp.float32)  111 us
    all_gather x2, waiting for transfers between devices, entering_2(): everything = jax.tree.map(lambda part: lax.all_gather(part, axis), shard)  77.5 us
    all_gather x1, waiting for transfers between devices, body(): full_rows = lax.all_gather(hidden, 'head', axis=2, tiled=True)  64.2 us
    another operation x41, other arithmetic  34.8 us
    unnamed x102, local copies, waits for them, and re-layouts  29.3 us
    psum x1, blocking collectives, body(): lax.psum((norm_gain_grad, gate_proj_grad, in_grad, step_proj_grad, kernel...  26.2 us
    dynamic_update_slice x26, local copies, waits for them, and re-layouts, body(): lax.map(partial(device_state, step_bias=step_bias, decay_log=decay_log),...  23.4 us
  transfers between devices with their start and end apart: 10, of which 5 were waited for; matrix products, arithmetic and copies ran while one was open for 21% of the time, Pallas kernels for 0%

commit v1 on v0

v1 whole, which is shorter than its diff:
```python
from functools import partial

import jax
import jax.numpy as jnp
from jax import lax
from jax.experimental import pallas as pl
from jax.experimental.pallas import tpu as pltpu
from jax.sharding import PartitionSpec as P

HEAD_DIM = 64
STATE = 128
CONV = 4
BLOCK = 256
EPS = 1e-05
EDGE = 8
PAD = 16

bf16 = jnp.bfloat16
f32 = jnp.float32

NN = (((1,), (0,)), ((), ()))
NT = (((1,), (1,)), ((), ()))
TN = (((0,), (0,)), ((), ()))


def dot(left, right, dims=NN):
    return lax.dot_general(left, right, dims, preferred_element_type=f32)


def parts_of(value, count):
    parts, rest = [], value
    for _ in range(count - 1):
        part = rest.astype(bf16)
        parts.append(part)
        rest = rest - part.astype(f32)
    parts.append(rest.astype(bf16))
    return parts


def head_map(heads, width):
    head = lax.broadcasted_iota(jnp.int32, (heads, width), 0)
    channel = lax.broadcasted_iota(jnp.int32, (heads, width), 1)
    return ((channel >> 6) == head).astype(bf16)


def spread(value, hmap, count=2):
    return sum(dot(part, hmap) for part in parts_of(value, count))


def per_head(value, hmap, count=2):
    return sum(dot(part, hmap, NT) for part in parts_of(value, count))


def triangle(lower):
    row = lax.broadcasted_iota(jnp.int32, (BLOCK, BLOCK), 0)
    col = lax.broadcasted_iota(jnp.int32, (BLOCK, BLOCK), 1)
    return (row >= col) if lower else (row <= col)


def running_sum(value, lower):
    tri = jnp.where(triangle(lower), 1.0, 0.0).astype(bf16)
    return sum(dot(tri, part) for part in parts_of(value, 3))


def sigmoid(value):
    return 1.0 / (1.0 + jnp.exp(-value))


def softplus(value):
    return jnp.maximum(value, 0.0) + jnp.log1p(jnp.exp(-jnp.abs(value)))


def silu_slope(value):
    sigma = sigmoid(value)
    return sigma * (1.0 + value * (1.0 - sigma))


def shifted_taps(source, taps, start, rows):
    return sum(taps[k : k + 1, :] * source[pl.ds(start + k, rows), :] for k in range(CONV))


def pack_state(out, state, decay):
    out[0, :STATE, :] = state.astype(bf16)
    high = decay.astype(bf16)
    rest = (decay - high.astype(f32)).astype(bf16)
    row = lax.broadcasted_iota(jnp.int32, (PAD, state.shape[1]), 0)
    tail = jnp.where(row == 0, high.astype(f32), jnp.where(row == 1, rest.astype(f32), 0.0))
    out[0, STATE:, :] = tail.astype(bf16)


def project_kernel(
    rows, edge, gain, gate_w, value_w, state_w, step_w, tap_v, bias_v, tap_s, bias_s, step_bias, decay_log,
    normed_o, inv_o, gate_o, cv_o, cs_o, mv_o, ms_o, x_o, b_o, c_o, raw_o, step_o, cum_o, cumt_o, stept_o,
    local_o, pack_o, ev_o, es_o,
    ext_v, ext_s, held, factor,
):
    j, last = pl.program_id(1), pl.num_programs(1) - 1
    heads, width = step_w.shape[1], value_w.shape[1]
    hmap = head_map(heads, width)

    def norm(block):
        block = block.astype(f32)
        inv = lax.rsqrt(jnp.mean(block * block, -1, keepdims=True) + EPS)
        return (block * inv * gain[...]).astype(bf16), inv

    @pl.when(j == 0)
    def _():
        before, _ = norm(edge[0])
        edge_v = dot(before, value_w[...])[PAD - EDGE :]
        edge_s = dot(before, state_w[...])[PAD - EDGE :]
        ext_v[:EDGE, :] = edge_v
        ext_s[:EDGE, :] = edge_s
        ev_o[0] = edge_v
        es_o[0] = edge_s
        held[...] = jnp.zeros_like(held)
        factor[...] = jnp.ones_like(factor)

    @pl.when(j > 0)
    def _():
        ext_v[:EDGE, :] = ext_v[BLOCK:, :]
        ext_s[:EDGE, :] = ext_s[BLOCK:, :]

    normed, inv = norm(rows[...])
    normed_o[...] = normed
    inv_o[...] = jnp.broadcast_to(inv, inv_o.shape)
    gate_o[...] = dot(normed, gate_w[...])
    conv_v = dot(normed, value_w[...])
    conv_s = dot(normed, state_w[...])
    raw = dot(normed, step_w[...])
    cv_o[...] = conv_v
    cs_o[...] = conv_s
    ext_v[EDGE:, :] = conv_v
    ext_s[EDGE:, :] = conv_s
    mixed_v = bias_v[...] + shifted_taps(ext_v, tap_v, EDGE - CONV + 1, BLOCK)
    mixed_s = bias_s[...] + shifted_taps(ext_s, tap_s, EDGE - CONV + 1, BLOCK)
    mv_o[...] = mixed_v
    ms_o[...] = mixed_s
    x = (mixed_v * sigmoid(mixed_v)).astype(bf16)
    maps = (mixed_s * sigmoid(mixed_s)).astype(bf16)
    x_o[...] = x
    b_o[...] = maps[:, :STATE]
    c_o[...] = maps[:, STATE:]

    step = softplus(raw + step_bias[...])
    cum = running_sum(-jnp.exp(decay_log[...]) * step, True)
    raw_o[...] = raw
    step_o[...] = step
    cum_o[...] = cum
    cumt_o[0] = cum.T
    stept_o[0] = step.T
    total = cum[BLOCK - 1 :]
    weights = jnp.exp(total - cum) * step
    x_weighted = (x.astype(f32) * spread(weights, hmap)).astype(bf16)
    local = dot(maps[:, :STATE], x_weighted, TN)
    local_o[0] = local
    decay = spread(jnp.exp(cum[BLOCK - 8 :]), hmap)[7:]
    held[...] = decay * held[...] + local
    factor[...] = decay * factor[...]

    @pl.when(j == last)
    def _():
        pack_state(pack_o, held[...], factor[...])


def within_kernel(x, b, c, cum, cumt, stept, skip, y_o):
    heads, width = cum.shape[1], x.shape[1]
    hmap = head_map(heads, width)
    causal = triangle(True)
    scores = dot(c[...], b[...], NT)
    left = lax.broadcasted_iota(jnp.int32, (BLOCK, 2 * HEAD_DIM), 1) < HEAD_DIM
    for pair in range(heads // 2):
        lanes = slice(pair * 2 * HEAD_DIM, (pair + 1) * 2 * HEAD_DIM)
        x_pair = x[:, lanes]
        inside = []
        for h in (2 * pair, 2 * pair + 1):
            spread_h = jnp.where(causal, cum[:, h : h + 1] - cumt[0, h : h + 1, :], -1e30)
            mixing = (scores * jnp.exp(spread_h) * stept[0, h : h + 1, :]).astype(bf16)
            inside.append(dot(mixing, x_pair))
        y_o[:, lanes] = jnp.where(left, inside[0], inside[1]) + skip[:, lanes] * x_pair.astype(f32)


def output_kernel(
    y, c, cum, local, entering, gate, cot, out_w, gate_gain, ssd_o, grad_o, starts_o, stats_o, state
):
    j = pl.program_id(1)
    heads, width = cum.shape[1], gate.shape[1]
    hmap = head_map(heads, width)

    @pl.when(j == 0)
    def _():
        state[...] = entering[0]

    start = state[...]
    starts_o[0] = start
    scale = spread(jnp.exp(cum[...]), hmap)
    ssd = y[...] + scale * dot(c[...], start.astype(bf16))
    state[...] = scale[BLOCK - 1 :] * start + local[0]
    ssd_o[...] = ssd
    gate_in = gate[...]
    gated = ssd * (gate_in * sigmoid(gate_in))
    grad = dot(cot[...], out_w[...], NT)
    grad_o[...] = grad
    ones = jnp.ones((8, width), bf16)

    def row_sum(value):
        return sum(dot(ones, part, NT) for part in parts_of(value, 3))

    first = lax.broadcasted_iota(jnp.int32, (8, BLOCK), 0) == 0
    stats_o[...] = jnp.where(first, row_sum(gated * gated), row_sum(grad * gate_gain[...] * gated))


def gate_kernel(
    inner, ssd, gate, grad, stats, gate_gain, skip, x, c, cum,
    normal_o, gssd_o, ggate_o, row_o, sgrad_o, sums_o, pack_o, held, factor,
):
    i, j, last = pl.program_id(0), pl.program_id(1), pl.num_programs(1) - 1
    heads, width = cum.shape[1], gate.shape[1]
    hmap = head_map(heads, width)

    @pl.when((i == 0) & (j == 0))
    def _():
        sums_o[...] = jnp.zeros_like(sums_o)

    @pl.when(j == 0)
    def _():
        held[...] = jnp.zeros_like(held)
        factor[...] = jnp.ones_like(factor)

    columns = stats[...].T
    inv_gate = lax.rsqrt(columns[:, 0:1] / inner + EPS)
    mean_dot = inv_gate * columns[:, 1:2] / inner
    gate_in, ssd_out = gate[...], ssd[...]
    sigma = sigmoid(gate_in)
    act = gate_in * sigma
    unit = ssd_out * act * inv_gate
    normal_o[...] = (unit * gate_gain[...]).astype(bf16)
    grad_normal = grad[...]
    grad_gated = inv_gate * (grad_normal * gate_gain[...] - unit * mean_dot)
    grad_ssd = (grad_gated * act).astype(bf16)
    gssd_o[...] = grad_ssd
    ggate_o[...] = (grad_gated * ssd_out * (sigma * (1.0 + gate_in * (1.0 - sigma)))).astype(bf16)
    grad_float, x_float = grad_ssd.astype(f32), x[...].astype(f32)
    row_o[...] = per_head(grad_float * (ssd_out - skip[...] * x_float), hmap)
    gain_sum = jnp.sum(grad_normal * unit, 0, keepdims=True)
    skip_sum = jnp.sum(grad_float * x_float, 0, keepdims=True)
    row = lax.broadcasted_iota(jnp.int32, (8, width), 0)
    sums_o[...] += jnp.where(row == 0, gain_sum, jnp.where(row == 1, skip_sum, 0.0))
    scale = spread(jnp.exp(cum[...]), hmap)
    scaled = (grad_float * scale).astype(bf16)
    state_grad = dot(c[...], scaled, TN)
    sgrad_o[0] = state_grad
    held[...] += factor[...] * state_grad
    factor[...] = factor[...] * scale[BLOCK - 1 :]

    @pl.when(j == last)
    def _():
        pack_state(pack_o, held[...], factor[...])


def score_kernel(x, b, c, cum, cumt, step, gssd, gx_o, gb_o, gc_o, total):
    heads = cum.shape[1]
    causal = triangle(False)
    scores = dot(b[...], c[...], NT)
    left = lax.broadcasted_iota(jnp.int32, (BLOCK, 2 * HEAD_DIM), 1) < HEAD_DIM
    zero = jnp.zeros((BLOCK, 2 * HEAD_DIM), bf16)
    for pair in range(heads // 2):
        lanes = slice(pair * 2 * HEAD_DIM, (pair + 1) * 2 * HEAD_DIM)
        x_pair, g_pair = x[:, lanes], gssd[:, lanes]
        inside = []
        for side in range(2):
            h = 2 * pair + side
            spread_h = jnp.where(causal, cumt[0, h : h + 1, :] - cum[:, h : h + 1], -1e30)
            damping = jnp.exp(spread_h) * step[:, h : h + 1]
            x_head = jnp.where(left, x_pair, zero) if side == 0 else jnp.where(left, zero, x_pair)
            low = (dot(x_head, g_pair, NT) * damping).astype(bf16).astype(f32)
            if h == 0:
                total[...] = low
            else:
                total[...] += low
            inside.append(dot((scores * damping).astype(bf16), g_pair))
        gx_o[:, lanes] = jnp.where(left, inside[0], inside[1])
    high, rest = parts_of(total[...], 2)
    gb_o[...] = dot(high, c[...]) + dot(rest, c[...])
    gc_o[...] = dot(high, b[...], TN) + dot(rest, b[...], TN)


def back_kernel(
    leaving, starts, sgrad, gx_in, gb_in, gc_in, row_term, x, gssd, b, c, raw, step, cum,
    mv, ms, cv, cs, ev, es, tap_v, tap_s, skip, step_bias, decay_log,
    gv_o, gs_o, tailv_o, tails_o, retv_o, rets_o, graw_o, sumv_o, sums_o, sumh_o,
    end, ext_v, ext_s, pre_v, pre_s,
):
    i, j, last = pl.program_id(0), pl.program_id(1), pl.num_programs(1) - 1
    heads, width = cum.shape[1], x.shape[1]
    hmap = head_map(heads, width)

    @pl.when((i == 0) & (j == 0))
    def _():
        sumv_o[...] = jnp.zeros_like(sumv_o)
        sums_o[...] = jnp.zeros_like(sums_o)
        sumh_o[...] = jnp.zeros_like(sumh_o)

    @pl.when(j == 0)
    def _():
        end[...] = leaving[0]
        ext_v[BLOCK:, :] = jnp.zeros((EDGE, ext_v.shape[1]), f32)
        ext_s[BLOCK:, :] = jnp.zeros((EDGE, ext_s.shape[1]), f32)

    @pl.when(j > 0)
    def _():
        ext_v[BLOCK:, :] = ext_v[:EDGE, :]
        ext_s[BLOCK:, :] = ext_s[:EDGE, :]

    end_grad = end[...]
    end_low = end_grad.astype(bf16)
    start = starts[0]
    cum_v, step_v = cum[...], step[...]
    x_float, g_float = x[...].astype(f32), gssd[...].astype(f32)
    remain = jnp.exp(cum_v[BLOCK - 1 :] - cum_v)
    weight = spread(remain * step_v, hmap)
    scale = spread(jnp.exp(cum_v), hmap)
    decay = scale[BLOCK - 1 :]
    grad_weighted = weight * dot(b[...], end_low)
    q_weight = per_head(x_float * grad_weighted, hmap)
    q_mixing = per_head(x_float * gx_in[...], hmap)
    grad_x = gx_in[...] + grad_weighted + skip[...] * g_float
    x_weighted = (x_float * weight).astype(bf16)
    grad_b = gb_in[...] + dot(x_weighted, end_low, NT)
    grad_c = gc_in[...] + dot((g_float * scale).astype(bf16), start.astype(bf16), NT)
    along = jnp.sum(end_grad * start, 0, keepdims=True) * decay
    grad_total = per_head(jnp.broadcast_to(along, (8, width)), hmap)[:1] + jnp.sum(q_weight, 0, keepdims=True)
    end[...] = decay * end_grad + sgrad[0]

    final = lax.broadcasted_iota(jnp.int32, (BLOCK, heads), 0) == BLOCK - 1
    grad_cum = row_term[...] - q_mixing - q_weight + jnp.where(final, grad_total, 0.0)
    grad_log = running_sum(grad_cum, False)
    rate = -jnp.exp(decay_log[...])
    shifted = raw[...] + step_bias[...]
    sigma = sigmoid(shifted)
    ratio = jnp.where(step_v > 0.0, sigma / jnp.where(step_v > 0.0, step_v, 1.0), 1.0)
    grad_raw = grad_log * rate * sigma + (q_mixing + q_weight) * ratio
    graw_o[...] = grad_raw.astype(bf16)
    bias_sum = jnp.sum(grad_raw, 0, keepdims=True)
    decay_sum = jnp.sum(grad_log * rate * step_v, 0, keepdims=True)
    row = lax.broadcasted_iota(jnp.int32, (8, heads), 0)
    sumh_o[...] += jnp.where(row == 0, bias_sum, jnp.where(row == 1, decay_sum, 0.0))

    ext_v[:BLOCK, :] = grad_x * silu_slope(mv[...])
    slope = silu_slope(ms[...])
    ext_s[:BLOCK, :STATE] = grad_b * slope[:, :STATE]
    ext_s[:BLOCK, STATE:] = grad_c * slope[:, STATE:]

    def back(ext, taps, conv, grad_o, tail_o, sum_o):
        grad = sum(taps[k : k + 1, :] * ext[pl.ds(CONV - 1 - k, BLOCK), :] for k in range(CONV))
        grad_o[...] = grad.astype(bf16)

        @pl.when(j == 0)
        def _():
            tail_o[0] = grad[BLOCK - PAD :]

        source = conv[...]
        lines = [
            jnp.sum(source * ext[pl.ds(CONV - 1 - k, BLOCK), :], 0, keepdims=True) for k in range(CONV)
        ]
        lines.append(jnp.sum(ext[:BLOCK, :], 0, keepdims=True))
        place = lax.broadcasted_iota(jnp.int32, sum_o.shape, 0)
        sum_o[...] += sum(jnp.where(place == k, line, 0.0) for k, line in enumerate(lines))

    back(ext_v, tap_v, cv, gv_o, tailv_o, sumv_o)
    back(ext_s, tap_s, cs, gs_o, tails_o, sums_o)

    def before(ext, pre, taps, edge, ret_o, sum_o):
        pre[:EDGE, :] = jnp.zeros((EDGE, pre.shape[1]), f32)
        pre[EDGE:, :] = ext[:EDGE, :]
        views = [pre[pl.ds(CONV - 1 - k, EDGE), :] for k in range(CONV)]
        ret_o[0] = sum(taps[k : k + 1, :] * views[k] for k in range(CONV))
        source = edge[0]
        place = lax.broadcasted_iota(jnp.int32, sum_o.shape, 0)
        sum_o[...] += sum(
            jnp.where(place == k, jnp.sum(source * views[k], 0, keepdims=True), 0.0) for k in range(CONV)
        )

    @pl.when(j == last)
    def _():
        before(ext_v, pre_v, tap_v, ev, retv_o, sumv_o)
        before(ext_s, pre_s, tap_s, es, rets_o, sums_o)


def call(kernel, grid, ins, outs, scratch=(), name=None):
    def spec(shape, index):
        return pl.BlockSpec(shape, index)

    return pl.pallas_call(
        kernel,
        grid=grid,
        in_specs=[spec(s, m) for _, s, m in ins],
        out_specs=[spec(s, m) for _, _, s, m in outs],
        out_shape=[jax.ShapeDtypeStruct(full, kind) for full, kind, _, _ in outs],
        scratch_shapes=[pltpu.VMEM(s, kind) for s, kind in scratch],
        compiler_params=pltpu.CompilerParams(dimension_semantics=("arbitrary",) * len(grid)),
        name=name,
    )(*[a for a, _, _ in ins])


def passed_along(block, axis, distance):
    devices = range(lax.axis_size(axis))
    route = [(i - distance, i) for i in devices if i - distance in devices]
    return lax.ppermute(block, axis, route)


def small_sum(value, axis):
    size = lax.axis_size(axis)
    total = value
    for distance in range(1, size):
        total = total + lax.ppermute(value, axis, [(i, (i + distance) % size) for i in range(size)])
    return total


def open_pack(packed):
    state = packed[:, :STATE].astype(f32)
    decay = packed[:, STATE].astype(f32) + packed[:, STATE + 1].astype(f32)
    return state, decay[:, None]


def close_pack(state, decay):
    high = lax.reduce_precision(decay, 8, 7)
    filler = jnp.zeros((state.shape[0], PAD - 2, state.shape[2]), bf16)
    return jnp.concatenate([state.astype(bf16), high.astype(bf16), (decay - high).astype(bf16), filler], 1)


def carried_in(packed, axis, reverse):
    size, index = lax.axis_size(axis), lax.axis_index(axis)
    total, total_decay = open_pack(packed)
    prefix, prefix_decay = jnp.zeros_like(total), jnp.ones_like(total_decay)
    distance = 1
    while distance < size:
        route = [(i, i ^ distance) for i in range(size)]
        other, other_decay = open_pack(lax.ppermute(packed, axis, route))
        upper = (index // distance) % 2 == 1
        behind = jnp.logical_not(upper) if reverse else upper
        prefix = jnp.where(behind, prefix_decay * other + prefix, prefix)
        prefix_decay = jnp.where(behind, prefix_decay * other_decay, prefix_decay)
        if 2 * distance < size:
            total = jnp.where(behind, total_decay * other + total, other_decay * total + other)
            total_decay = total_decay * other_decay
            packed = close_pack(total, total_decay)
        distance *= 2
    return prefix


def body(
    hidden,
    norm_gain,
    gate_proj,
    value_proj,
    state_proj,
    step_proj,
    conv_value,
    conv_value_bias,
    conv_state,
    conv_state_bias,
    step_bias,
    decay_log,
    skip_gain,
    gate_gain,
    out_proj,
    cotangent,
):
    batch, tokens, part = hidden.shape
    head_index = lax.axis_index("head")
    ranks = lax.axis_size("head")
    features = norm_gain.shape[0]
    width, heads = value_proj.shape[1], step_proj.shape[1]
    maps = 2 * STATE
    blocks = tokens // BLOCK
    rows = batch * tokens
    count = batch * blocks
    grid = (batch, blocks)

    def row(block_width):
        return (BLOCK, block_width), lambda i, j: (i * blocks + j, 0)

    def back_row(block_width):
        return (BLOCK, block_width), lambda i, j: (i * blocks + blocks - 1 - j, 0)

    def fixed(array):
        rank = array.ndim
        return (array, array.shape, lambda i, j: (0,) * rank)

    def per_block(*tail):
        return (1,) + tail, lambda i, j: (i * blocks + j,) + (0,) * len(tail)

    def back_block(*tail):
        return (1,) + tail, lambda i, j: (i * blocks + blocks - 1 - j,) + (0,) * len(tail)

    def per_batch(*tail):
        return (1,) + tail, lambda i, j: (i,) + (0,) * len(tail)

    def lead(vector):
        return vector[None, :]

    full_rows = lax.all_gather(hidden, "head", axis=2, tiled=True)
    cot_rows = lax.all_gather(cotangent, "head", axis=2, tiled=True).reshape(rows, features)
    edge = passed_along(full_rows[:, tokens - PAD :], "seq", 1)
    full_rows = full_rows.reshape(rows, features)
    skip = lead(jnp.repeat(skip_gain, HEAD_DIM))
    bias, rate = lead(step_bias), lead(decay_log)
    gain = lead(gate_gain)

    def out(full, kind, block):
        return (full, kind) + block

    (
        normed, inv_rms, gate_in, conv_v, conv_s, mixed_v, mixed_s, x, b, c, raw, step, cum, cumt, stept,
        local, packed, edge_v, edge_s,
    ) = call(
        project_kernel,
        grid,
        [
            (full_rows,) + row(features),
            (edge,) + per_batch(PAD, features),
            fixed(lead(norm_gain)),
            fixed(gate_proj),
            fixed(value_proj),
            fixed(state_proj),
            fixed(step_proj),
            fixed(conv_value),
            fixed(lead(conv_value_bias)),
            fixed(conv_state),
            fixed(lead(conv_state_bias)),
            fixed(bias),
            fixed(rate),
        ],
        [
            out((rows, features), bf16, row(features)),
            out((rows, 128), f32, row(128)),
            out((rows, width), f32, row(width)),
            out((rows, width), f32, row(width)),
            out((rows, maps), f32, row(maps)),
            out((rows, width), f32, row(width)),
            out((rows, maps), f32, row(maps)),
            out((rows, width), bf16, row(width)),
            out((rows, STATE), bf16, row(STATE)),
            out((rows, STATE), bf16, row(STATE)),
            out((rows, heads), f32, row(heads)),
            out((rows, heads), f32, row(heads)),
            out((rows, heads), f32, row(heads)),
            out((count, heads, BLOCK), f32, per_block(heads, BLOCK)),
            out((count, heads, BLOCK), f32, per_block(heads, BLOCK)),
            out((count, STATE, width), f32, per_block(STATE, width)),
            out((batch, STATE + PAD, width), bf16, per_batch(STATE + PAD, width)),
            out((batch, EDGE, width), f32, per_batch(EDGE, width)),
            out((batch, EDGE, maps), f32, per_batch(EDGE, maps)),
        ],
        [
            ((EDGE + BLOCK, width), f32),
            ((EDGE + BLOCK, maps), f32),
            ((STATE, width), f32),
            ((1, width), f32),
        ],
        name="project",
    )
    entering = carried_in(packed, "seq", False)
    (y,) = call(
        within_kernel,
        grid,
        [
            (x,) + row(width),
            (b,) + row(STATE),
            (c,) + row(STATE),
            (cum,) + row(heads),
            (cumt,) + per_block(heads, BLOCK),
            (stept,) + per_block(heads, BLOCK),
            fixed(skip),
        ],
        [out((rows, width), f32, row(width))],
        name="within",
    )
    ssd_out, grad_normal, starts, stats = call(
        output_kernel,
        grid,
        [
            (y,) + row(width),
            (c,) + row(STATE),
            (cum,) + row(heads),
            (local,) + per_block(STATE, width),
            (entering,) + per_batch(STATE, width),
            (gate_in,) + row(width),
            (cot_rows,) + row(features),
            fixed(out_proj),
            fixed(gain),
        ],
        [
            out((rows, width), f32, row(width)),
            out((rows, width), f32, row(width)),
            out((count, STATE, width), f32, per_block(STATE, width)),
            ((8, rows), f32, (8, BLOCK), lambda i, j: (0, i * blocks + j)),
        ],
        [((STATE, width), f32)],
        name="output",
    )
    stats = small_sum(stats, "head")
    normal_gated, grad_ssd, grad_gate_in, row_term, state_grads, gate_sums, packed_back = call(
        partial(gate_kernel, float(width * ranks)),
        grid,
        [
            (ssd_out,) + row(width),
            (gate_in,) + row(width),
            (grad_normal,) + row(width),
            (stats, (8, BLOCK), lambda i, j: (0, i * blocks + j)),
            fixed(gain),
            fixed(skip),
            (x,) + row(width),
            (c,) + row(STATE),
            (cum,) + row(heads),
        ],
        [
            out((rows, width), bf16, row(width)),
            out((rows, width), bf16, row(width)),
            out((rows, width), bf16, row(width)),
            out((rows, heads), f32, row(heads)),
            out((count, STATE, width), f32, per_block(STATE, width)),
            ((8, width), f32, (8, width), lambda i, j: (0, 0)),
            out((batch, STATE + PAD, width), bf16, per_batch(STATE + PAD, width)),
        ],
        [((STATE, width), f32), ((1, width), f32)],
        name="gate",
    )
    leaving = carried_in(packed_back, "seq", True)
    grad_x_in, grad_b_in, grad_c_in = call(
        score_kernel,
        grid,
        [
            (x,) + row(width),
            (b,) + row(STATE),
            (c,) + row(STATE),
            (cum,) + row(heads),
            (cumt,) + per_block(heads, BLOCK),
            (step,) + row(heads),
            (grad_ssd,) + row(width),
        ],
        [
            out((rows, width), f32, row(width)),
            out((rows, STATE), f32, row(STATE)),
            out((rows, STATE), f32, row(STATE)),
        ],
        [((BLOCK, BLOCK), f32)],
        name="score",
    )
    partial_out = dot(normal_gated, out_proj).astype(bf16).reshape(batch, tokens, features)
    out_part = lax.psum_scatter(partial_out, "head", scatter_dimension=2, tiled=True)
    block_out = (hidden.astype(f32) + out_part.astype(f32)).astype(bf16)
    out_proj_grad = lax.psum(dot(normal_gated, cot_rows, TN).astype(bf16), "seq")
    gate_proj_part = dot(normed, grad_gate_in, TN).astype(bf16)
    gate_proj_grad = lax.psum(gate_proj_part, "seq")

    (
        grad_conv_v, grad_conv_s, tail_v, tail_s, ret_v, ret_s, grad_raw, sum_v, sum_s, sum_h,
    ) = call(
        back_kernel,
        grid,
        [
            (leaving,) + per_batch(STATE, width),
            (starts,) + back_block(STATE, width),
            (state_grads,) + back_block(STATE, width),
            (grad_x_in,) + back_row(width),
            (grad_b_in,) + back_row(STATE),
            (grad_c_in,) + back_row(STATE),
            (row_term,) + back_row(heads),
            (x,) + back_row(width),
            (grad_ssd,) + back_row(width),
            (b,) + back_row(STATE),
            (c,) + back_row(STATE),
            (raw,) + back_row(heads),
            (step,) + back_row(heads),
            (cum,) + back_row(heads),
            (mixed_v,) + back_row(width),
            (mixed_s,) + back_row(maps),
            (conv_v,) + back_row(width),
            (conv_s,) + back_row(maps),
            (edge_v,) + per_batch(EDGE, width),
            (edge_s,) + per_batch(EDGE, maps),
            fixed(conv_value),
            fixed(conv_state),
            fixed(skip),
            fixed(bias),
            fixed(rate),
        ],
        [
            out((rows, width), bf16, back_row(width)),
            out((rows, maps), bf16, back_row(maps)),
            out((batch, PAD, width), f32, per_batch(PAD, width)),
            out((batch, PAD, maps), f32, per_batch(PAD, maps)),
            out((batch, EDGE, width), f32, per_batch(EDGE, width)),
            out((batch, EDGE, maps), f32, per_batch(EDGE, maps)),
            out((rows, heads), bf16, back_row(heads)),
            ((8, width), f32, (8, width), lambda i, j: (0, 0)),
            ((8, maps), f32, (8, maps), lambda i, j: (0, 0)),
            ((8, heads), f32, (8, heads), lambda i, j: (0, 0)),
        ],
        [
            ((STATE, width), f32),
            ((BLOCK + EDGE, width), f32),
            ((BLOCK + EDGE, maps), f32),
            ((2 * EDGE, width), f32),
            ((2 * EDGE, maps), f32),
        ],
        name="back",
    )
    back_edge = passed_along(jnp.concatenate([ret_v, ret_s], 2), "seq", -1)

    def mended(grad, tail, given):
        lower = (tail[:, PAD - EDGE :] + given).astype(bf16)
        tail = jnp.concatenate([tail[:, : PAD - EDGE].astype(bf16), lower], 1)
        grad = grad.reshape(batch, tokens, -1)
        return lax.dynamic_update_slice(grad, tail, (0, tokens - PAD, 0)).reshape(rows, -1)

    grad_conv_v = mended(grad_conv_v, tail_v, back_edge[..., :width])
    grad_conv_s = mended(grad_conv_s, tail_s, back_edge[..., width:])

    grad_normed = (
        dot(grad_gate_in, gate_proj, NT)
        + dot(grad_conv_v, value_proj, NT)
        + dot(grad_conv_s, state_proj, NT)
        + dot(grad_raw, step_proj, NT)
    ).astype(bf16)
    grad_part = lax.psum_scatter(
        grad_normed.reshape(batch, tokens, features), "head", scatter_dimension=2, tiled=True
    ).astype(f32)

    value_part = dot(normed, grad_conv_v, TN).astype(bf16)
    state_part = dot(normed, grad_conv_s, TN).astype(bf16)
    step_part = dot(normed, grad_raw, TN)
    value_proj_grad = lax.psum(value_part, "seq")
    state_proj_grad = lax.psum(state_part, ("seq", "head"))

    def along(left, right):
        return jnp.sum(left.astype(f32) * right, -1)

    row_dot = along(grad_gate_in, gate_in) + along(grad_conv_v, conv_v) + along(grad_conv_s, conv_s)
    row_dot = (row_dot + along(grad_raw, raw)) / features
    row_dot = lax.psum(row_dot, "head").reshape(batch, tokens, 1)

    inv = inv_rms[:, :1].reshape(batch, tokens, 1)
    unit = hidden.astype(f32) * inv
    norm_part = jnp.sum(grad_part * unit, (0, 1))
    gain_part = lax.dynamic_slice_in_dim(norm_gain, head_index * part, part)
    grad_input = inv * (grad_part * gain_part - unit * row_dot)
    hidden_grad = (cotangent.astype(f32) + grad_input).astype(bf16)

    sum_s = lax.psum(sum_s, "head")
    totals = lax.psum(
        (norm_part, step_part, sum_v, sum_s, sum_h, gate_sums),
        "seq",
    )
    norm_gain_grad, step_proj_grad, sum_v, sum_s, sum_h, gate_sums = totals
    return (
        block_out,
        hidden_grad,
        norm_gain_grad,
        gate_proj_grad.astype(f32),
        value_proj_grad.astype(f32),
        state_proj_grad.astype(f32),
        step_proj_grad,
        sum_v[:CONV],
        sum_v[CONV],
        sum_s[:CONV],
        sum_s[CONV],
        sum_h[0],
        sum_h[1],
        jnp.sum(gate_sums[1].reshape(heads, HEAD_DIM), -1),
        gate_sums[0],
        out_proj_grad.astype(f32),
    )


def solution(mesh):
    placed = (
        P(None, "seq", "head"),
        P(),
        P(None, "head"),
        P(None, "head"),
        P(),
        P(None, "head"),
        P(None, "head"),
        P("head"),
        P(),
        P(),
        P("head"),
        P("head"),
        P("head"),
        P("head"),
        P("head", None),
        P(None, "seq", "head"),
    )
    return jax.shard_map(
        body,
        mesh=mesh,
        in_specs=placed,
        out_specs=(
            P(None, "seq", "head"),
            P(None, "seq", "head"),
            P("head"),
            P(None, "head"),
            P(None, "head"),
            P(),
            P(None, "head"),
            P(None, "head"),
            P("head"),
            P(),
            P(),
            P("head"),
            P("head"),
            P("head"),
            P("head"),
            P("head", None),
        ),
        check_vma=False,
    )
```

time: 959 us -> 671 us (0.70)
  local copies, waits for them, and re-layouts: 165 us -> 47.9 us
  matrix products: 145 us -> 34 us
  other arithmetic: 132 us -> 30.7 us
  Pallas kernels: 0 us -> 77.7 us
  waiting for transfers between devices: 428 us -> 401 us
  blocking collectives: 58.2 us -> 41 us
  starting transfers between devices: 3.58 us -> 15.1 us
    unnamed x9, waiting for transfers between devices: 1.48 us -> 114 us
    dot_general x38 -> x10, matrix products: 145 us -> 34 us  [dot(): return lax.dot_general(left, right, dims, preferred_element_type=f32)]
    psum x3, waiting for transfers between devices: 285 us -> 192 us  [the longest x1 113 us: body(): gate_proj_grad = lax.psum(gate_proj_part, 'seq')]
    pallas_call x0 -> x6, Pallas kernels: none -> 77.7 us  [call(): pl.pallas_call(kernel, grid=grid, in_specs=[spec(s, m) for _, s, m in ins...]
    all_gather x3 -> x1, waiting for transfers between devices: 77.5 us -> 3.13 us  [body(): lax.all_gather(cotangent, 'head', axis=2, tiled=True)]
    another operation x41 -> x0, other arithmetic: 34.8 us -> none
    dynamic_update_slice x32 -> x0, local copies, waits for them, and re-layouts: 29.8 us -> none  [the longest x26 23.4 us: body(): lax.map(partial(device_state, step_bias=step_bias, decay_log=decay_log),...]
    ppermute x0 -> x9, waiting for transfers between devices: none -> 26.1 us  [the longest x6 21.8 us: carried_in(): other, other_decay = open_pack(lax.ppermute(packed, axis, route))]
  transfers between devices with their start and end apart: 10 -> 18, of which waited for: 5 -> 16; matrix products, arithmetic and copies ran while one was open for 21% -> 15% of each run, Pallas kernels for 0% -> 6%
where the time goes in v1:
time: 671 us; the launch traced here: 663 us
  waiting for transfers between devices  401 us (60%)
  Pallas kernels  77.7 us (12%)
  local copies, waits for them, and re-layouts  47.9 us (7%)
  blocking collectives  41 us (6%)
  matrix products  34 us (5%)
  other arithmetic  30.7 us (5%)
  starting transfers between devices  15.1 us (2%)
  between operations  15 us (2%)
    unnamed x9, waiting for transfers between devices  114 us
    psum x1, waiting for transfers between devices, body(): gate_proj_grad = lax.psum(gate_proj_part, 'seq')  113 us
    pallas_call x6, Pallas kernels, call(): pl.pallas_call(kernel, grid=grid, in_specs=[spec(s, m) for _, s, m in ins...  77.7 us
    all_gather x1, waiting for transfers between devices, body(): full_rows = lax.all_gather(hidden, 'head', axis=2, tiled=True)  66.8 us
    psum x1, waiting for transfers between devices, body(): state_proj_grad = lax.psum(state_part, ('seq', 'head'))  59.1 us
    unnamed x87, local copies, waits for them, and re-layouts  37.3 us
    dot_general x10, matrix products, dot(): return lax.dot_general(left, right, dims, preferred_element_type=f32)  34 us
    psum x1, blocking collectives, body(): lax.psum((norm_part, step_part, sum_v, sum_s, sum_h, gate_sums), 'seq')  24.2 us
  transfers between devices with their start and end apart: 18, of which 16 were waited for; matrix products, arithmetic and copies ran while one was open for 15% of the time, Pallas kernels for 6%

profile of v1, /device:TPU:0, one launch (start us, length us, event | category | flops | bytes accessed | tf_op | source)
XLA Modules:
  0.0 662.8 jit_solution(7256258826927215519)
XLA Ops:
  8.7 66.8 %all-gather.3.cloned.1.call-done = bf16[2,512,1536]{2,1,0:T(8,128)(2,1)} async-done(((bf16[2,512,384]{2,1,0:T(8,128)(2,1)}), bf16[2,512,1536]{2,1,0:T(8,128)(2,1)}) %all-gather.3.cloned.1.call-update) | async-done | bytes 3145744 | tf_op jit(solution)/shard_map/all_gather | solution.py:502
  83.0 21.3 %project.1 = (bf16[1024,1536]{1,0:T(8,128)(2,1)}, f32[1024,128]{1,0:T(8,128)}, f32[1024,768]{1,0:T(8,128)}, f32[1024,768]{1,0:T(8,128)}, f32[1024,256]{1,0:T(8,1...) custom-call(bf16[1024,1536]{1,0:T(8,128)(2,1)} %bitcast.85, ...), custom_call_target="tpu_custom_call" | custom-call | tf_op jit(solution)/shard_map/project/pallas_call | solution.py:393
  111.4 10.9 %collective-permute-done.2 = bf16[2,144,768]{2,1,0:T(8,128)(2,1)S(1)} collective-permute-done((bf16[2,144,768]{2,1,0:T(8,128)(2,1)S(1)}, bf16[2,144,768]{2,1,0:T(8,128)(2,1)S(1)}, u32[]{:S(2)}, u32[]{:S(2)}) %collective-permute-start.2) | collective-permute-done | bytes 442400 | tf_op jit(solution)/shard_map/ppermute | solution.py:438
  125.8 6.5 within.1.y
  139.0 11.1 %output.1 = (f32[1024,768]{1,0:T(8,128)}, f32[1024,768]{1,0:T(8,128)}, f32[4,128,768]{2,1,0:T(8,128)}, f32[8,1024]{1,0:T(8,128)}) custom-call(f32[1024,768]{1,0:T(8,128)} %within.1.y, bf16[1024,128]{1,0:T(8,128)(2,1)} %get-tuple-element.61.c, f32[1024,12]{1,0:T(8,128)} %get-tuple-element.62.cum, f32[4,128,768]{2,1,0:T(8,128)} %get-tuple-element.65.local, ...), custom_call_target="tpu_custom_call" | custom-call | tf_op jit(solution)/shard_map/output/pallas_call | solution.py:393
  159.4 10.9 %gate.1 = (bf16[1024,768]{1,0:T(8,128)(2,1)}, bf16[1024,768]{1,0:T(8,128)(2,1)}, bf16[1024,768]{1,0:T(8,128)(2,1)}, f32[1024,12]{1,0:T(8,128)}, f32[4,128,768]{2...) custom-call(f32[1024,768]{1,0:T(8,128)} %get-tuple-element.68.ssd, f32[1024,768]{1,0:T(8,128)} %get-tuple-element.67.gate, ...), custom_call_target="tpu_custom_call" | custom-call | tf_op jit(solution)/shard_map/gate/pallas_call | solution.py:393
  176.2 9.8 %score.1 = (f32[1024,768]{1,0:T(8,128)}, f32[1024,128]{1,0:T(8,128)}, f32[1024,128]{1,0:T(8,128)}) custom-call(bf16[1024,768]{1,0:T(8,128)(2,1)} %get-tuple-element.59.x, bf16[1024,128]{1,0:T(8,128)(2,1)} %get-tuple-element.60.b, bf16[1024,128]{1,0:T(8,128)(2,1)} %get-tuple-element.61.c, f32[1024,12]{1,0:T(8,128)} %get-tuple-element.62.cum, ...), custom_call_target="tpu_custom_call" | custom-call | tf_op jit(solution)/shard_map/score/pallas_call | solution.py:393
  189.0 5.7 convolution_convert_fusion.1
  200.0 18.0 %back.1 = (bf16[1024,768]{1,0:T(8,128)(2,1)}, bf16[1024,256]{1,0:T(8,128)(2,1)}, f32[2,16,768]{2,1,0:T(8,128)}, f32[2,16,256]{2,1,0:T(8,128)}, f32[2,8,768]{2,1,...) custom-call(f32[2,128,768]{2,1,0:T(8,128)} %add_select_fusion.leavin, ...), custom_call_target="tpu_custom_call" | custom-call | tf_op jit(solution)/shard_map/back/pallas_call | solution.py:393
  220.4 5.4 convolution_convert_fusion.3
  229.2 5.4 convolution_convert_fusion.2
  236.3 5.4 convolution_convert_fusion
  241.7 7.1 %copy.35 = bf16[2,512,1536]{1,0,2:T(2,128)(2,1)S(1)} copy(bf16[2,512,1536]{2,1,0:T(8,128)(2,1)} %bitcast.89) | data formatting | bytes 6291456
  252.8 4.3 fusion.31
  262.9 5.8 copy.37
  268.7 4.5 copy.52
  282.2 16.9 %all-reduce.1 = (f32[2,512]{1,0:T(2,128)S(1)}, f32[8,256]{1,0:T(8,128)S(1)}) all-reduce(f32[2,512]{1,0:T(2,128)S(1)} %mul.264, f32[8,256]{1,0:T(8,128)S(1)} %copy-done.28), channel_id=1, replica_groups=mesh['seq'=8,'head'=4] {'head'}, use_global_device_ids=true, to_apply=%region_6.7 | all-reduce | flops 3072 | bytes 24576 | tf_op jit(solution)/shard_map/psum | solution.py:742
  299.0 59.1 %all-reduce.7.cloned.1.call-done = bf16[1536,256]{1,0:T(8,128)(2,1)} async-done(((bf16[1536,256]{1,0:T(8,128)(2,1)}), bf16[1536,256]{1,0:T(8,128)(2,1)}) %all-reduce.7.cloned.1.call-update) | async-done | bytes 786448 | tf_op jit(solution)/shard_map/psum | solution.py:735
  360.5 112.8 %all-reduce.11.cloned.1.call-done = (bf16[1536,768]{1,0:T(8,128)(2,1)}, bf16[1536,768]{1,0:T(8,128)(2,1)}, bf16[768,1536]{1,0:T(8,128)(2,1)}) async-done(((bf16[1536,768]{1,0:T(8,128)(2,1)}, bf16[1536,768]{1,0:T(8,128)(2,1)}, bf16[768,1536]{1,0:T(8,128)(2,1)}), (bf16[1536,768]{1,0:T(8,128)(2,1)}, bf16[1536,768]{1,0:T(8,128)(2,1)}, bf16[768,1536]{1,0:T(8,128)(2,1)})) %all-reduce.11.cloned.1.call-update) | async-done | bytes 7077904 | tf_op jit(solution)/shard_map/psum | solution.py:655
  473.3 4.4 convert_element_type.300
  483.1 53.0 %reduce-scatter.7.cloned.1.call-done = bf16[384,1024]{1,0:T(8,128)(2,1)} async-done(((bf16[1536,1024]{1,0:T(8,128)(2,1)}), bf16[384,1024]{1,0:T(8,128)(2,1)}) %reduce-scatter.7.cloned.1.call-update) | async-done | bytes 786448
  539.3 59.2 %reduce-scatter.9.cloned.1.call-done = bf16[384,1024]{1,0:T(8,128)(2,1)} async-done(((bf16[1536,1024]{1,0:T(8,128)(2,1)}), bf16[384,1024]{1,0:T(8,128)(2,1)}) %reduce-scatter.9.cloned.1.call-update) | async-done | bytes 786448
  606.0 24.2 %all-reduce = (f32[384]{0:T(512)}, f32[8,768]{1,0:T(8,128)S(1)}, f32[8,256]{1,0:T(8,128)S(1)}, f32[8,12]{1,0:T(8,128)S(1)}, f32[8,768]{1,0:T(8,128)S(1)}) all-reduce(f32[384]{0:T(512)S(1)} %get-tuple-element.128, f32[8,768]{1,0:T(8,128)S(1)} %copy-done.26, ...), channel_id=1, replica_groups=mesh['seq'=8,'head'=4] {'seq'}, use_global_device_ids=true, to_apply=%region_8.9 | all-reduce | flops 14816 | bytes 118528 | tf_op jit(solution)/shard_map/psum | solution.py:752
  634.4 19.8 %all-reduce.9.cloned.1.call-done = f32[1536,12]{0,1:T(8,128)} async-done(((f32[1536,12]{0,1:T(8,128)}), f32[1536,12]{0,1:T(8,128)}) %all-reduce.9.cloned.1.call-update) | async-done | bytes 73744 | tf_op jit(solution)/shard_map/psum | solution.py:752
  (180 shorter events, 99.4 us)
Async XLA Ops:
  7.2 68.4 %all-gather.3.cloned.1.call-start = ((), (), s32[]{:S(2)}) async-start(), calls=%async_computation.2 | async-start | bytes 3932160 | tf_op jit(solution)/shard_map/all_gather | solution.py:502
  7.9 131.1 %all-gather.5.cloned.1.call-start = ((), (), s32[]{:S(2)}) async-start(), calls=%async_computation.3 | async-start | bytes 3932160 | tf_op jit(solution)/shard_map/all_gather | solution.py:503
  8.7 349.5 %all-reduce.7.cloned.1.call-start = ((), (), s32[]{:S(2)}) async-start(), calls=%async_computation.4 | async-start | bytes 1572864 | tf_op jit(solution)/shard_map/psum | solution.py:735
  76.4 5.9 collective-permute-start
  104.3 18.2 %copy-start.20 = (bf16[2,144,768]{2,1,0:T(8,128)(2,1)S(1)}, bf16[2,144,768]{2,1,0:T(8,128)(2,1)}, u32[]{:S(2)}) copy-start(bf16[2,144,768]{2,1,0:T(8,128)(2,1)} %get-tuple-element.66) | copy-start | bytes 1327108
  104.3 3.3 collective-permute-start.1
  108.5 16.1 %copy-start.30 = (f32[768]{0:T(1024)S(1)}, f32[768]{0:T(1024)}, u32[]{:S(2)}) copy-start(f32[768]{0:T(1024)} %param.29) | copy-start | bytes 9220
  108.5 16.6 %copy-start.31 = (f32[12]{0:T(128)S(1)}, f32[12]{0:T(128)}, u32[]{:S(2)}) copy-start(f32[12]{0:T(128)} %param.28) | copy-start | bytes 148
  109.9 12.5 %collective-permute-start.2 = (bf16[2,144,768]{2,1,0:T(8,128)(2,1)S(1)}, bf16[2,144,768]{2,1,0:T(8,128)(2,1)S(1)}, u32[]{:S(2)}, u32[]{:S(2)}) collective-permute-start(bf16[2,144,768]{2,1,0:T(8,128)(2,1)S(1)} %maximum_maximum_fusion), channel_id=1, source_target_pairs={{0,8},{4,12},{8,0},{12,4},{16,24},{20,28},{24,16},{28,20},{1,9},{5... | collective-permute-start | bytes 1327112 | tf_op jit(solution)/shard_map/ppermute | solution.py:438
  122.9 11.8 %collective-permute-start.3 = (bf16[2,144,768]{2,1,0:T(8,128)(2,1)S(1)}, bf16[2,144,768]{2,1,0:T(8,128)(2,1)S(1)}, u32[]{:S(2)}, u32[]{:S(2)}) collective-permute-start(bf16[2,144,768]{2,1,0:T(8,128)(2,1)S(1)} %maximum_maximum_fusion.1), channel_id=1, source_target_pairs={{0,16},{4,20},{8,24},{12,28},{16,0},{20,4},{24,8},{28,12},{1,17},{... | collective-permute-start | bytes 1327112 | tf_op jit(solution)/shard_map/ppermute | solution.py:438
  150.1 4.2 collective-permute-start.6
  151.1 5.7 collective-permute-start.5
  151.6 6.4 collective-permute-start.4
  170.3 2.1 collective-permute-start.7
  174.6 12.3 %collective-permute-start.8 = (bf16[2,144,768]{2,1,0:T(8,128)(2,1)S(1)}, bf16[2,144,768]{2,1,0:T(8,128)(2,1)S(1)}, u32[]{:S(2)}, u32[]{:S(2)}) collective-permute-start(bf16[2,144,768]{2,1,0:T(8,128)(2,1)S(1)} %maximum_maximum_fusion.2), channel_id=1, source_target_pairs={{0,8},{4,12},{8,0},{12,4},{16,24},{20,28},{24,16},{28,20},{1,9},{5... | collective-permute-start | bytes 1327112 | tf_op jit(solution)/shard_map/ppermute | solution.py:438
  187.5 11.4 %collective-permute-start.9 = (bf16[2,144,768]{2,1,0:T(8,128)(2,1)S(1)}, bf16[2,144,768]{2,1,0:T(8,128)(2,1)S(1)}, u32[]{:S(2)}, u32[]{:S(2)}) collective-permute-start(bf16[2,144,768]{2,1,0:T(8,128)(2,1)S(1)} %maximum_maximum_fusion.3), channel_id=1, source_target_pairs={{0,16},{4,20},{8,24},{12,28},{16,0},{20,4},{24,8},{28,12},{1,17},{... | collective-permute-start | bytes 1327112 | tf_op jit(solution)/shard_map/ppermute | solution.py:438
  200.0 20.3 %copy-start.2 = (bf16[1024,1536]{1,0:T(8,128)(2,1)S(1)}, bf16[1024,1536]{1,0:T(8,128)(2,1)}, u32[]{:S(2)}) copy-start(bf16[1024,1536]{1,0:T(8,128)(2,1)} %get-tuple-element.97) | copy-start | bytes 9437188
  218.8 6.9 %collective-permute-start.10 = (f32[2,8,1024]{2,1,0:T(8,128)S(1)}, f32[2,8,1024]{2,1,0:T(8,128)S(1)}, u32[]{:S(2)}, u32[]{:S(2)}) collective-permute-start(f32[2,8,1024]{2,1,0:T(8,128)S(1)} %pad_maximum_fusion), channel_id=1, source_target_pairs={{4,0},{8,4},{12,8},{16,12},{20,16},{24,20},{28,24},{5,1},{9,5},{13... | collective-permute-start | bytes 196616 | tf_op jit(solution)/shard_map/ppermute | solution.py:408
  228.6 244.8 %all-reduce.11.cloned.1.call-start = ((), (), s32[]{:S(2)}) async-start(), calls=%async_computation.8 | async-start | bytes 14155776 | tf_op jit(solution)/shard_map/psum | solution.py:655
  234.6 301.4 %reduce-scatter.7.cloned.1.call-start = ((), (), s32[]{:S(2)}) async-start(), calls=%async_computation.6 | async-start | bytes 3932160
  251.4 347.1 %reduce-scatter.9.cloned.1.call-start = ((), (), s32[]{:S(2)}) async-start(), calls=%async_computation.7 | async-start | bytes 3932160
  273.2 381.0 %all-reduce.9.cloned.1.call-start = ((), (), s32[]{:S(2)}) async-start(), calls=%async_computation.5 | async-start | bytes 196608 | tf_op jit(solution)/shard_map/psum | solution.py:752
  538.6 64.3 %copy-start.9 = (bf16[2,512,384]{2,1,0:T(8,128)(2,1)S(1)}, bf16[2,512,384]{2,1,0:T(8,128)(2,1)}, u32[]{:S(2)}) copy-start(bf16[2,512,384]{2,1,0:T(8,128)(2,1)} %param.16) | copy-start | bytes 2359300
  538.6 64.3 %copy-start.10 = (bf16[2,512,384]{2,1,0:T(8,128)(2,1)S(1)}, bf16[2,512,384]{2,1,0:T(8,128)(2,1)}, u32[]{:S(2)}) copy-start(bf16[2,512,384]{2,1,0:T(8,128)(2,1)} %param.31) | copy-start | bytes 2359300
  (27 other events, 86.2 us)
Sparse Core Ops, SparseCore 0:
  9.6 65.9 all-gather.2
  77.1 61.8 all-gather.4
  228.7 129.3 all-reduce.6
  361.6 111.6 all-reduce.10
  475.5 60.4 reduce-scatter.6
  538.2 60.3 reduce-scatter.8
  602.2 51.9 all-reduce.8
